TPU v7x, 256 devices: a whole 4x4x8 slice. The times are simulated.
256 devices in a mesh: seg: 8 (over y, core), ep: 32 (over z, x).
Axes of the slice: x: 4, y: 4, z: 8, core: 2. Of those that a mesh axis runs over, the one named last changes fastest.
Arguments:
- queries: bfloat16 [16384, 8192], P(('seg', 'ep')), may hold values from -6 to 6
- keys: bfloat16 [16384, 8192], P(('seg', 'ep')), may hold values from -1.25 to 1.25
- values: bfloat16 [16384, 8192], P(('seg', 'ep')), may hold values from -54 to 54
- log_decay: float32 [16384, 64], P('seg', 'ep'), may hold values from -1 to 0
- out_gain: float32 [8192], replicated, may hold values from 0.1 to 1.9
- out_proj: bfloat16 [8192, 6144], P('ep', 'seg'), may hold values from -0.0625 to 0.0625
- experts: int32 [2048, 2], P(('seg', 'ep')), may hold values from 0 to 15, all different within a row; in each aligned block of 8 rows (0 to 7, 8 to 15, ...) at most 2 rows name the same one
- gates: float32 [2048, 2], P(('seg', 'ep')), may hold values from 0.2 to 1
- up_weight: bfloat16 [32, 6144, 2304], P('ep', None, 'seg'), may hold values from -0.078125 to 0.078125
- down_weight: bfloat16 [32, 2304, 6144], P('ep', 'seg'), may hold values from -0.09375 to 0.09375
Outputs:
- attn_out: bfloat16 [16384, 8192], P(('seg', 'ep'))
- moe_out: bfloat16 [2048, 6144], P(('seg', 'ep'))
Inputs may be any that keep to these rules, and one draw needn't show every extreme that they name: Each row names two different experts. The 8 rows of one device name any one expert at most 2 times, and in some devices one expert exactly 2 times.
All inputs are finite; a program needn't handle non-finite values.
Results may differ from a plain program's by a relative error of at most 0.025.
Values may be sent and summed in bfloat16 or wider, within the bound.
No kernel may reach another device: no remote copies, remote signals or barrier semaphores. Data moves between devices by JAX's collectives and lax.ppermute only.
A program may use at most 128 MiB of HBM per device.

v0:
```python
import math
import jax
import jax.numpy as jnp
from jax import lax
from jax.sharding import Mesh
from jax.sharding import PartitionSpec as P

EP = ("ep_0", "ep_1")
SEG_EP = ("seg", "ep_0", "ep_1")
epsilon = 1e-06


def side_by_side(arrays, axis, dim, along):
    columns = [a.reshape(*a.shape[:along], -1) for a in arrays]
    both = jnp.concatenate(columns, axis=along)
    whole, at, done = (lax.all_gather(both, axis, axis=dim, tiled=True), 0, [])
    for a, column in zip(arrays, columns):
        section = whole[..., at : at + column.shape[along]]
        done.append(section.reshape(*section.shape[:along], *a.shape[along:]))
        at += column.shape[along]
    return tuple(done)


def sent_to_all(x, axis):
    devices = lax.axis_size(axis)
    return lax.all_to_all(jnp.broadcast_to(x[None], (devices, *x.shape)), axis, 0, 0, tiled=True)


def taken_together(x, axis):
    return sent_to_all(x, axis).sum(axis=0)


def scatter_axes(x, axes, dim):
    for axis in axes:
        x = lax.psum_scatter(x, axis, scatter_dimension=dim, tiled=True)
    return x


def route_tables(experts, gates, expert_count, capacity):
    token_count = experts.shape[0]
    flattened = experts.reshape(-1)
    onehot = (flattened[:, None] == jnp.arange(expert_count, dtype=jnp.int32)[None, :]).astype(
        jnp.int32
    )
    earlier = jnp.cumsum(onehot, axis=0) - onehot
    position = jnp.sum(earlier * onehot, axis=1)
    slot_index = (flattened * capacity + position).reshape(token_count, 2)
    columns = jnp.arange(expert_count * capacity, dtype=jnp.int32)
    matches = slot_index[:, :, None] == columns[None, None, :]
    dispatch = jnp.any(matches, axis=1).T.astype(jnp.bfloat16)
    combine = jnp.sum(jnp.where(matches, gates[:, :, None], 0.0), axis=1)
    return (dispatch, combine)


def expert_output(row_data, up_piece, down_piece):
    hidden = jax.nn.silu(jnp.dot(row_data, up_piece, preferred_element_type=jnp.float32)).astype(
        jnp.bfloat16
    )
    return jnp.dot(hidden, down_piece, preferred_element_type=jnp.float32)


def on_device(
    queries, keys, values, log_decay, out_gain, out_proj, experts, gates, up_weight, down_weight
):
    ep_count = lax.axis_size(EP)
    heads_local = log_decay.shape[1]
    head_dim = queries.shape[1] // (heads_local * ep_count)
    query_heads, key_heads, value_heads = (
        lax.all_to_all(queries, EP, split_axis=1, concat_axis=0, tiled=True),
        lax.all_to_all(keys, EP, split_axis=1, concat_axis=0, tiled=True),
        lax.all_to_all(values, EP, split_axis=1, concat_axis=0, tiled=True),
    )
    seg_length = query_heads.shape[0]
    query_heads = query_heads.reshape(seg_length, heads_local, head_dim)
    key_heads = key_heads.reshape(seg_length, heads_local, head_dim)
    value_heads = value_heads.reshape(seg_length, heads_local, head_dim)
    cumulative = jnp.cumsum(log_decay, axis=0)
    across = cumulative.T
    block_size = math.gcd(seg_length, 512)
    starts = jnp.arange(seg_length // block_size, dtype=jnp.int32) * block_size
    token_positions = jnp.arange(seg_length, dtype=jnp.int32)

    def block_mix(start):
        query_block = lax.dynamic_slice_in_dim(query_heads, start, block_size, 0)
        cum_block = lax.dynamic_slice_in_dim(across, start, block_size, 1)
        row_ids = start + jnp.arange(block_size, dtype=jnp.int32)
        causal = (row_ids[:, None] >= token_positions[None, :])[None]
        log_gap = cum_block[:, :, None] - across[:, None, :]
        weight = jnp.where(causal, jnp.exp(jnp.where(causal, log_gap, 0.0)), 0.0)
        scores = jnp.einsum(
            "thd,shd->hts", query_block, key_heads, preferred_element_type=jnp.float32
        )
        mixing = (scores * weight).astype(jnp.bfloat16)
        return jnp.einsum("hts,she->the", mixing, value_heads, preferred_element_type=jnp.float32)

    inside = lax.map(block_mix, starts).reshape(seg_length, heads_local, head_dim)
    ending = cumulative[-1]
    to_end = jnp.exp(ending[None, :] - cumulative)
    key_float = key_heads.astype(jnp.float32)
    value_float = value_heads.astype(jnp.float32)
    local_state = jnp.einsum("sh,shd,she->hde", to_end, key_float, value_float)
    all_ends, all_states = tuple(
        (
            part.astype(jnp.float32)
            for part in side_by_side(
                (ending[None].astype(jnp.bfloat16), local_state[None].astype(jnp.bfloat16)),
                "seg",
                0,
                2,
            )
        )
    )
    own_group = lax.axis_index("seg")
    group_ids = jnp.arange(all_ends.shape[0], dtype=jnp.int32)
    before = (group_ids < own_group)[:, None]
    through = jnp.cumsum(all_ends, axis=0)
    reaching = jnp.sum(jnp.where(before, all_ends, 0.0), axis=0)
    factors = jnp.where(before, jnp.exp(jnp.where(before, reaching[None, :] - through, 0.0)), 0.0)
    carried = jnp.einsum("gh,ghde->hde", factors, all_states)
    outside = jnp.exp(cumulative)[:, :, None] * jnp.einsum(
        "thd,hde->the", query_heads.astype(jnp.float32), carried
    )
    mixture = (inside + outside).astype(jnp.bfloat16).reshape(seg_length, heads_local * head_dim)
    token_mix = lax.all_to_all(mixture, EP, split_axis=0, concat_axis=1, tiled=True)
    as_float = token_mix.astype(jnp.float32)
    inv_rms = lax.rsqrt(jnp.mean(as_float * as_float, axis=1, keepdims=True) + epsilon)
    attn_out = (as_float * inv_rms * out_gain[None, :]).astype(jnp.bfloat16)
    row_stride = 8
    own_width = heads_local * head_dim
    feature_count = own_width * ep_count
    picked_float = mixture.reshape(seg_length // row_stride, row_stride, own_width)[:, 0].astype(
        jnp.float32
    )
    square_sums = taken_together(jnp.sum(picked_float * picked_float, axis=1), EP)
    picked_rms = lax.rsqrt(square_sums[:, None] / feature_count + epsilon)
    gain_slice = lax.dynamic_slice_in_dim(out_gain, lax.axis_index(EP) * own_width, own_width, 0)
    normed_rows = (picked_float * picked_rms * gain_slice[None, :]).astype(jnp.bfloat16)
    proj_terms = jnp.dot(
        normed_rows,
        lax.all_gather(out_proj, "seg", axis=1, tiled=True),
        preferred_element_type=jnp.float32,
    )
    moe_in = (
        scatter_axes(proj_terms.astype(jnp.bfloat16), EP, 0)
        .astype(jnp.float32)
        .astype(jnp.bfloat16)
    )
    expert_count = ep_count // 2
    token_count, model_width = moe_in.shape
    capacity = max(2, 4 * token_count // expert_count)
    dispatch, combine = route_tables(experts, gates, expert_count, capacity)
    up_piece = up_weight[0]
    down_piece = down_weight[0]
    slot_rows = jnp.dot(dispatch, moe_in, preferred_element_type=jnp.float32).astype(jnp.bfloat16)
    outgoing = jnp.repeat(slot_rows.reshape(expert_count, capacity, model_width), 2, axis=0)
    arrived = lax.all_to_all(outgoing, EP, split_axis=0, concat_axis=0, tiled=True).reshape(
        ep_count * capacity, model_width
    )
    gathered = lax.all_gather(arrived, "seg", axis=0, tiled=True)
    owned_sums = lax.psum_scatter(
        expert_output(gathered, up_piece, down_piece).astype(jnp.bfloat16),
        "seg",
        scatter_dimension=0,
        tiled=True,
    ).astype(jnp.float32)
    returned_back = lax.all_to_all(
        owned_sums.reshape(ep_count, capacity, model_width).astype(jnp.bfloat16),
        EP,
        split_axis=0,
        concat_axis=0,
        tiled=True,
    ).astype(jnp.float32)
    paired = returned_back.reshape(expert_count, 2, capacity, model_width)
    halves = (paired[:, 0] + paired[:, 1]).reshape(expert_count * capacity, model_width)
    summed = jnp.dot(combine, halves)
    moe_out = summed.astype(jnp.bfloat16)
    return (attn_out, moe_out)


def solution(mesh):
    torus = Mesh(mesh.devices.reshape(mesh.shape["seg"], 8, 4), ("seg", "ep_0", "ep_1"))
    placed = (
        P(SEG_EP, None),
        P(SEG_EP, None),
        P(SEG_EP, None),
        P("seg", EP),
        P(),
        P(EP, "seg"),
        P(SEG_EP, None),
        P(SEG_EP, None),
        P(EP, None, "seg"),
        P(EP, "seg", None),
    )
    return jax.shard_map(
        on_device,
        mesh=torus,
        in_specs=placed,
        out_specs=(P(SEG_EP, None), P(SEG_EP, None)),
        check_vma=False,
    )
```

profile of v0, /device:TPU:2, one launch (start us, length us, event | category | flops | bytes accessed | tf_op | source)
XLA Modules:
  0.0 520.2 jit_solution(4376102759249833830)
XLA Ops:
  7.2 2.5 copy.199
  9.7 11.8 %all-to-all-start.1 = ((bf16[64,32,256]{2,0,1:T(8,128)(2,1)}), bf16[64,32,256]{2,0,1:T(8,128)(2,1)}, u32[]{:S(2)}, u32[]{:S(2)}) async-start(bf16[64,32,256]{2,0,1:T(8,128)(2,1)} %bitcast.112), calls=%async_computation.1 | async-start | bytes 2097152 | tf_op jit(solution)/shard_map/all_to_all | solution.py:70
  21.5 2.3 copy.198
  23.8 25.8 %all-to-all-done.1 = bf16[64,32,256]{2,0,1:T(8,128)(2,1)} async-done(((bf16[64,32,256]{2,0,1:T(8,128)(2,1)}), bf16[64,32,256]{2,0,1:T(8,128)(2,1)}, u32[]{:S(2)}, u32[]{:S(2)}) %all-to-all-start.1) | async-done | bytes 1048608 | tf_op jit(solution)/shard_map/all_to_all | solution.py:70
  49.6 5.6 %all-to-all-start.2 = ((bf16[64,32,256]{2,0,1:T(8,128)(2,1)}), bf16[64,32,256]{2,0,1:T(8,128)(2,1)}, u32[]{:S(2)}, u32[]{:S(2)}) async-start(bf16[64,32,256]{2,0,1:T(8,128)(2,1)} %bitcast.110), calls=%async_computation.2 | async-start | bytes 2097152 | tf_op jit(solution)/shard_map/all_to_all | solution.py:71
  64.1 2.3 copy.200
  67.8 2.2 reshape.156
  70.0 12.2 %all-to-all-done.2 = bf16[64,32,256]{2,0,1:T(8,128)(2,1)} async-done(((bf16[64,32,256]{2,0,1:T(8,128)(2,1)}), bf16[64,32,256]{2,0,1:T(8,128)(2,1)}, u32[]{:S(2)}, u32[]{:S(2)}) %all-to-all-start.2) | async-done | bytes 1048608 | tf_op jit(solution)/shard_map/all_to_all | solution.py:71
  82.3 5.6 %all-to-all-start = ((bf16[64,32,256]{2,0,1:T(8,128)(2,1)}), bf16[64,32,256]{2,0,1:T(8,128)(2,1)}, u32[]{:S(2)}, u32[]{:S(2)}) async-start(bf16[64,32,256]{2,0,1:T(8,128)(2,1)} %bitcast.111), calls=%async_computation | async-start | bytes 2097152 | tf_op jit(solution)/shard_map/all_to_all | solution.py:69
  87.9 2.2 reshape.159
  90.1 5.6 %convert_multiply_fusion.1 = bf16[2048,2,128]{2,1,0:T(2,128)(2,1)S(1)} fusion(bf16[2048,2,128]{2,1,0:T(2,128)(2,1)} %reshape.156, f32[2048,2]{1,0:T(8,128)} %copy.139), kind=kLoop, calls=%fused_computation.27 | loop fusion | flops 1572864 | bytes 2113536 | tf_op jit(solution)/shard_map/sh,shd,she->hde/dot_general | solution.py:101
  95.7 2.5 fusion.18
  100.7 13.8 %all_gather.9 = bf16[8,2,16385]{2,1,0:T(2,128)(2,1)S(1)} all-gather(bf16[1,2,16385]{2,1,0:T(2,128)(2,1)S(1)} %pad_maximum_fusion), channel_id=1, replica_groups=mesh['seg'=8,'ep_0'=8,'ep_1'=4] {'seg'}, dimensions={0}, use_global_device_ids=true | all-gather | bytes 589860 | tf_op jit(solution)/shard_map/all_gather | solution.py:16
  116.0 2.4 copy.136
  120.3 2.2 reshape.163
  122.6 2.1 reshape.155
  124.7 2.3 copy.135
  127.0 99.5 %while.11 = (s32[]{:T(128)}, f32[4,512,2,128]{1,0,3,2:T(4,128)}, s32[4]{0:T(128)S(1)}, bf16[2048,2,128]{2,0,1:T(8,128)(2,1)}, bf16[2048,2,128]{2,0,1:T(8,128)(2,...) while((s32[]{:T(128)}, f32[4,512,2,128]{1,0,3,2:T(4,128)}, ...), condition=%wide.region_3.4_spmd.clone, body=%wide.region_2.3_spmd.clone.sunk | while | flops 1085276672 | bytes 7110819 | solution.py:96
  132.3 6.6 %fusion.58 = f32[1,512,2,128]{3,1,2,0:T(8,128)} fusion(bf16[2048,2,128]{2,0,1:T(8,128)(2,1)} %get-tuple-element.204, bf16[2048,2,128]{2,0,1:T(8,128)(2,1)} %get-tuple-element.202, f32[2,2048]{1,0:T(2,128)} %get-tuple-element.203, f32[2,512]{1,0:T(2,128)S(1)} %constant_dynamic-slice_fusion.2, pred[512,2048]{1,0:T(8,128)(4,1)} %iota_compare_fusion.5, ...), kind=kOutput, calls=%fused_computation.4.clone.1 | convolution fusion | flops 1084227584 | bytes 3952644 | tf_op jit(solution)/shard_map/while/body/eval_jaxpr/hts,she->the/dot_general | solution.py:94
  140.8 11.1 %dynamic_update_slice.6 = f32[4,512,2,128]{1,0,3,2:T(4,128)} dynamic-update-slice(f32[4,512,2,128]{1,0,3,2:T(4,128)} %get-tuple-element.189, f32[1,512,2,128]{1,0,3,2:T(1,128)} %copy.204, s32[]{:T(128)} %get-tuple-element.188, s32[]{:T(128)} %constant.22.clone.1..sunk, s32[]{:T(128)} %constant.22.clone.1..sunk, s32[]{:T(128)} %constant.22.clone.1..sunk) | dynamic-update-slice | bytes 1048580 | tf_op jit(solution)/shard_map/while/body/jit(dynamic_update_index_in_dim)/dynamic_update_slice | solution.py:96
  157.2 6.6 %fusion.58 = f32[1,512,2,128]{3,1,2,0:T(8,128)} fusion(bf16[2048,2,128]{2,0,1:T(8,128)(2,1)} %get-tuple-element.204, bf16[2048,2,128]{2,0,1:T(8,128)(2,1)} %get-tuple-element.202, f32[2,2048]{1,0:T(2,128)} %get-tuple-element.203, f32[2,512]{1,0:T(2,128)S(1)} %constant_dynamic-slice_fusion.2, pred[512,2048]{1,0:T(8,128)(4,1)} %iota_compare_fusion.5, ...), kind=kOutput, calls=%fused_computation.4.clone.1 | convolution fusion | flops 1084227584 | bytes 3952644 | tf_op jit(solution)/shard_map/while/body/eval_jaxpr/hts,she->the/dot_general | solution.py:94
  165.7 11.1 %dynamic_update_slice.6 = f32[4,512,2,128]{1,0,3,2:T(4,128)} dynamic-update-slice(f32[4,512,2,128]{1,0,3,2:T(4,128)} %get-tuple-element.189, f32[1,512,2,128]{1,0,3,2:T(1,128)} %copy.204, s32[]{:T(128)} %get-tuple-element.188, s32[]{:T(128)} %constant.22.clone.1..sunk, s32[]{:T(128)} %constant.22.clone.1..sunk, s32[]{:T(128)} %constant.22.clone.1..sunk) | dynamic-update-slice | bytes 1048580 | tf_op jit(solution)/shard_map/while/body/jit(dynamic_update_index_in_dim)/dynamic_update_slice | solution.py:96
  182.0 6.6 %fusion.58 = f32[1,512,2,128]{3,1,2,0:T(8,128)} fusion(bf16[2048,2,128]{2,0,1:T(8,128)(2,1)} %get-tuple-element.204, bf16[2048,2,128]{2,0,1:T(8,128)(2,1)} %get-tuple-element.202, f32[2,2048]{1,0:T(2,128)} %get-tuple-element.203, f32[2,512]{1,0:T(2,128)S(1)} %constant_dynamic-slice_fusion.2, pred[512,2048]{1,0:T(8,128)(4,1)} %iota_compare_fusion.5, ...), kind=kOutput, calls=%fused_computation.4.clone.1 | convolution fusion | flops 1084227584 | bytes 3952644 | tf_op jit(solution)/shard_map/while/body/eval_jaxpr/hts,she->the/dot_general | solution.py:94
  190.5 11.1 %dynamic_update_slice.6 = f32[4,512,2,128]{1,0,3,2:T(4,128)} dynamic-update-slice(f32[4,512,2,128]{1,0,3,2:T(4,128)} %get-tuple-element.189, f32[1,512,2,128]{1,0,3,2:T(1,128)} %copy.204, s32[]{:T(128)} %get-tuple-element.188, s32[]{:T(128)} %constant.22.clone.1..sunk, s32[]{:T(128)} %constant.22.clone.1..sunk, s32[]{:T(128)} %constant.22.clone.1..sunk) | dynamic-update-slice | bytes 1048580 | tf_op jit(solution)/shard_map/while/body/jit(dynamic_update_index_in_dim)/dynamic_update_slice | solution.py:96
  206.9 6.6 %fusion.58 = f32[1,512,2,128]{3,1,2,0:T(8,128)} fusion(bf16[2048,2,128]{2,0,1:T(8,128)(2,1)} %get-tuple-element.204, bf16[2048,2,128]{2,0,1:T(8,128)(2,1)} %get-tuple-element.202, f32[2,2048]{1,0:T(2,128)} %get-tuple-element.203, f32[2,512]{1,0:T(2,128)S(1)} %constant_dynamic-slice_fusion.2, pred[512,2048]{1,0:T(8,128)(4,1)} %iota_compare_fusion.5, ...), kind=kOutput, calls=%fused_computation.4.clone.1 | convolution fusion | flops 1084227584 | bytes 3952644 | tf_op jit(solution)/shard_map/while/body/eval_jaxpr/hts,she->the/dot_general | solution.py:94
  215.4 11.1 %dynamic_update_slice.6 = f32[4,512,2,128]{1,0,3,2:T(4,128)} dynamic-update-slice(f32[4,512,2,128]{1,0,3,2:T(4,128)} %get-tuple-element.189, f32[1,512,2,128]{1,0,3,2:T(1,128)} %copy.204, s32[]{:T(128)} %get-tuple-element.188, s32[]{:T(128)} %constant.22.clone.1..sunk, s32[]{:T(128)} %constant.22.clone.1..sunk, s32[]{:T(128)} %constant.22.clone.1..sunk) | dynamic-update-slice | bytes 1048580 | tf_op jit(solution)/shard_map/while/body/jit(dynamic_update_index_in_dim)/dynamic_update_slice | solution.py:96
  226.5 3.7 reshape.160
  233.2 3.4 fusion.14
  236.6 3.7 copy.145
  240.3 2.5 reshape_reshape.3
  245.6 9.8 %all-to-all-start.4 = ((f32[32,1,256]{2,1,0:T(1,128)}), f32[32,1,256]{2,1,0:T(1,128)}, u32[]{:S(2)}, u32[]{:S(2)}) async-start(f32[32,1,256]{2,1,0:T(1,128)} %broadcast_in_dim.85), calls=%async_computation.4 | async-start | bytes 65536 | tf_op jit(solution)/shard_map/all_to_all | solution.py:26
  256.3 7.8 %all-to-all-done.4 = f32[32,1,256]{2,1,0:T(1,128)} async-done(((f32[32,1,256]{2,1,0:T(1,128)}), f32[32,1,256]{2,1,0:T(1,128)}, u32[]{:S(2)}, u32[]{:S(2)}) %all-to-all-start.4) | async-done | bytes 32800 | tf_op jit(solution)/shard_map/all_to_all | solution.py:26
  265.0 4.7 convolution_convert_fusion.1
  269.8 41.9 %reduce-scatter.4.cloned.1.call-done = bf16[32,6144]{1,0:T(8,128)(2,1)} async-done(((bf16[256,6144]{1,0:T(8,128)(2,1)}), bf16[32,6144]{1,0:T(8,128)(2,1)}) %reduce-scatter.4.cloned.1.call-update) | async-done | bytes 393232 | tf_op jit(solution)/shard_map/reduce_scatter | solution.py:35
  315.2 19.9 %reduce-scatter.6.cloned.1.call-done = bf16[8,6144]{1,0:T(8,128)(2,1)} async-done(((bf16[32,6144]{1,0:T(8,128)(2,1)}), bf16[8,6144]{1,0:T(8,128)(2,1)}) %reduce-scatter.6.cloned.1.call-update) | async-done | bytes 98320 | tf_op jit(solution)/shard_map/reduce_scatter | solution.py:35
  337.0 2.0 reshape.164
  340.4 30.7 %all_to_all.77 = bf16[32,2,6144]{2,1,0:T(2,128)(2,1)} all-to-all(bf16[32,2,6144]{2,1,0:T(2,128)(2,1)S(1)} %bitcast.113), channel_id=1, replica_groups=mesh['seg'=8,'ep_0'=8,'ep_1'=4] {'ep_0','ep_1'}, dimensions={0} | all-to-all | bytes 1572864 | tf_op jit(solution)/shard_map/all_to_all | solution.py:156
  371.2 3.0 reshape.166
  374.2 40.3 %all-gather.5.cloned.1.call-done = bf16[512,6144]{1,0:T(8,128)(2,1)} async-done(((bf16[64,6144]{1,0:T(8,128)(2,1)}), bf16[512,6144]{1,0:T(8,128)(2,1)}) %all-gather.5.cloned.1.call-update) | async-done | bytes 6291472 | tf_op jit(solution)/shard_map/all_gather | solution.py:159
  414.5 12.0 %convolution_convert_fusion = bf16[512,6144]{1,0:T(8,128)(2,1)} fusion(bf16[1,288,6144]{2,1,0:T(8,128)(2,1)S(1)} %copy-done, bf16[512,6144]{1,0:T(8,128)(2,1)} %all-gather.5.cloned.1.call-done, bf16[1,6144,288]{1,2,0:T(8,128)(2,1)} %param.20), kind=kOutput, calls=%fused_computation.10 | convolution fusion | flops 3627761664 | bytes 19660800 | tf_op jit(solution)/shard_map/dot_general | solution.py:59
  426.6 2.5 all_to_all.65
  429.1 10.2 %all-to-all-start.3 = ((bf16[32,64,256]{2,1,0:T(8,128)(2,1)}), bf16[32,64,256]{2,1,0:T(8,128)(2,1)}, u32[]{:S(2)}, u32[]{:S(2)}) async-start(bf16[32,64,256]{2,1,0:T(8,128)(2,1)} %all_to_all.65), calls=%async_computation.3 | async-start | bytes 2097152 | tf_op jit(solution)/shard_map/all_to_all | solution.py:124
  439.4 28.5 %all-to-all-done.3 = bf16[32,64,256]{2,1,0:T(8,128)(2,1)} async-done(((bf16[32,64,256]{2,1,0:T(8,128)(2,1)}), bf16[32,64,256]{2,1,0:T(8,128)(2,1)}, u32[]{:S(2)}, u32[]{:S(2)}) %all-to-all-start.3) | async-done | bytes 1048608 | tf_op jit(solution)/shard_map/all_to_all | solution.py:124
  472.5 2.9 convert_element_type.93
  475.3 9.8 %all-to-all-start.6 = ((bf16[32,2,6144]{2,1,0:T(2,128)(2,1)}), bf16[32,2,6144]{2,1,0:T(2,128)(2,1)}, u32[]{:S(2)}, u32[]{:S(2)}) async-start(bf16[32,2,6144]{2,1,0:T(2,128)(2,1)} %convert_element_type.93), calls=%async_computation.9 | async-start | bytes 1572864 | tf_op jit(solution)/shard_map/all_to_all | solution.py:166
  485.2 2.8 multiply_convert_fusion.1
  488.0 18.8 %all-to-all-done.6 = bf16[32,2,6144]{2,1,0:T(2,128)(2,1)} async-done(((bf16[32,2,6144]{2,1,0:T(2,128)(2,1)}), bf16[32,2,6144]{2,1,0:T(2,128)(2,1)}, u32[]{:S(2)}, u32[]{:S(2)}) %all-to-all-start.6) | async-done | bytes 786464 | tf_op jit(solution)/shard_map/all_to_all | solution.py:166
  506.8 2.0 convert.7
  (98 shorter events, 62.2 us)
Async XLA Ops:
  7.2 407.3 %copy-start = (bf16[1,288,6144]{2,1,0:T(8,128)(2,1)S(1)}, bf16[1,288,6144]{2,1,0:T(8,128)(2,1)}, u32[]{:S(2)}) copy-start(bf16[1,288,6144]{2,1,0:T(8,128)(2,1)} %param.21) | copy-start | bytes 10616836
  9.7 46.3 %copy-start.4 = (f32[2048,2]{0,1:T(2,128)S(1)}, f32[2048,2]{0,1:T(2,128)}, u32[]{:S(2)}) copy-start(f32[2048,2]{0,1:T(2,128)} %param.15) | copy-start | bytes 49156
  9.7 39.9 %all-to-all-start.1 = ((bf16[64,32,256]{2,0,1:T(8,128)(2,1)}), bf16[64,32,256]{2,0,1:T(8,128)(2,1)}, u32[]{:S(2)}, u32[]{:S(2)}) async-start(bf16[64,32,256]{2,0,1:T(8,128)(2,1)} %bitcast.112), calls=%async_computation.1 | async-start | bytes 2097152 | tf_op jit(solution)/shard_map/all_to_all | solution.py:70
  49.6 32.7 %all-to-all-start.2 = ((bf16[64,32,256]{2,0,1:T(8,128)(2,1)}), bf16[64,32,256]{2,0,1:T(8,128)(2,1)}, u32[]{:S(2)}, u32[]{:S(2)}) async-start(bf16[64,32,256]{2,0,1:T(8,128)(2,1)} %bitcast.110), calls=%async_computation.2 | async-start | bytes 2097152 | tf_op jit(solution)/shard_map/all_to_all | solution.py:71
  55.2 209.8 %all-gather.3.cloned.1.call-start = ((), (), s32[]{:S(2)}) async-start(), calls=%async_computation.10 | async-start | bytes 3538944 | tf_op jit(solution)/shard_map/all_gather | solution.py:140
  82.3 40.3 %all-to-all-start = ((bf16[64,32,256]{2,0,1:T(8,128)(2,1)}), bf16[64,32,256]{2,0,1:T(8,128)(2,1)}, u32[]{:S(2)}, u32[]{:S(2)}) async-start(bf16[64,32,256]{2,0,1:T(8,128)(2,1)} %bitcast.111), calls=%async_computation | async-start | bytes 2097152 | tf_op jit(solution)/shard_map/all_to_all | solution.py:69
  99.6 18.7 %copy-start.1 = (bf16[2048,2,128]{2,1,0:T(2,128)(2,1)S(1)}, bf16[2048,2,128]{2,1,0:T(2,128)(2,1)}, u32[]{:S(2)}) copy-start(bf16[2048,2,128]{2,1,0:T(2,128)(2,1)} %reshape.159) | copy-start | bytes 3145732
  119.6 7.4 %copy-start.7 = (bf16[8,2,1]{0,1,2:T(2,128)(2,1)}, bf16[8,2,1]{0,1,2:T(2,128)(2,1)S(1)}, u32[]{:S(2)}) copy-start(bf16[8,2,1]{0,1,2:T(2,128)(2,1)S(1)} %copy.159) | copy-start | bytes 100
  226.5 6.7 %copy-start.3 = (f32[2048,2]{0,1:T(2,128)S(1)}, f32[2048,2]{0,1:T(2,128)}, u32[]{:S(2)}) copy-start(f32[2048,2]{0,1:T(2,128)} %get-tuple-element.131) | copy-start | bytes 49156
  244.2 0.7 copy-start.2
  245.6 18.5 %all-to-all-start.4 = ((f32[32,1,256]{2,1,0:T(1,128)}), f32[32,1,256]{2,1,0:T(1,128)}, u32[]{:S(2)}, u32[]{:S(2)}) async-start(f32[32,1,256]{2,1,0:T(1,128)} %broadcast_in_dim.85), calls=%async_computation.4 | async-start | bytes 65536 | tf_op jit(solution)/shard_map/all_to_all | solution.py:26
  255.5 56.2 %reduce-scatter.4.cloned.1.call-start = ((), (), s32[]{:S(2)}) async-start(), calls=%async_computation.11 | async-start | bytes 3538944 | tf_op jit(solution)/shard_map/reduce_scatter | solution.py:35
  269.7 42.3 %copy-start.5 = (s32[8,2]{0,1:T(2,128)S(1)}, s32[8,2]{0,1:T(2,128)}, u32[]{:S(2)}) copy-start(s32[8,2]{0,1:T(2,128)} %param.18) | copy-start | bytes 196
  269.7 65.3 %reduce-scatter.6.cloned.1.call-start = ((), (), s32[]{:S(2)}) async-start(), calls=%async_computation.12 | async-start | bytes 491520 | tf_op jit(solution)/shard_map/reduce_scatter | solution.py:35
  311.7 102.8 %all-gather.5.cloned.1.call-start = ((), (), s32[]{:S(2)}) async-start(), calls=%async_computation.13 | async-start | bytes 7077888 | tf_op jit(solution)/shard_map/all_gather | solution.py:159
  374.1 98.3 %reduce-scatter.8.cloned.1.call-start = ((), (), s32[]{:S(2)}) async-start(), calls=%async_computation.14 | async-start | bytes 7077888 | tf_op jit(solution)/shard_map/reduce_scatter | solution.py:160
  426.6 12.8 %copy-start.6 = (f32[8,2]{0,1:T(2,128)S(1)}, f32[8,2]{0,1:T(2,128)}, u32[]{:S(2)}) copy-start(f32[8,2]{0,1:T(2,128)} %param.19) | copy-start | bytes 196
  429.1 38.7 %all-to-all-start.3 = ((bf16[32,64,256]{2,1,0:T(8,128)(2,1)}), bf16[32,64,256]{2,1,0:T(8,128)(2,1)}, u32[]{:S(2)}, u32[]{:S(2)}) async-start(bf16[32,64,256]{2,1,0:T(8,128)(2,1)} %all_to_all.65), calls=%async_computation.3 | async-start | bytes 2097152 | tf_op jit(solution)/shard_map/all_to_all | solution.py:124
  475.3 31.5 %all-to-all-start.6 = ((bf16[32,2,6144]{2,1,0:T(2,128)(2,1)}), bf16[32,2,6144]{2,1,0:T(2,128)(2,1)}, u32[]{:S(2)}, u32[]{:S(2)}) async-start(bf16[32,2,6144]{2,1,0:T(2,128)(2,1)} %convert_element_type.93), calls=%async_computation.9 | async-start | bytes 1572864 | tf_op jit(solution)/shard_map/all_to_all | solution.py:166
Sparse Core Ops, SparseCore 0:
  57.9 31.4 all-gather.2
  269.8 41.8 reduce-scatter.3
  314.2 20.7 reduce-scatter.5
  374.2 40.2 all-gather.4
  426.7 45.5 reduce-scatter.7
where the time goes:
time: 524 us; the launch traced here: 520 us
  waiting for transfers between devices  196 us (37%)
  local copies, waits for them, and re-layouts  115 us (22%)
  matrix products  54.1 us (10%)
  starting transfers between devices  53.3 us (10%)
  blocking collectives  44.5 us (8%)
  other arithmetic  36.2 us (7%)
  between operations  14 us (3%)
  loops' own time  6.62 us (1%)
    reduce_scatter x2, waiting for transfers between devices, scatter_axes(): x = lax.psum_scatter(x, axis, scatter_dimension=dim, tiled=True)  61.8 us
    dynamic_update_slice x8, local copies, waits for them, and re-layouts, on_device(): lax.map(block_mix, starts).reshape(seg_length, heads_local, head_dim)  52.2 us
    all_gather x1, waiting for transfers between devices, on_device(): gathered = lax.all_gather(arrived, 'seg', axis=0, tiled=True)  40.3 us
    all_to_all x1, blocking collectives, on_device(): lax.all_to_all(outgoing, EP, split_axis=0, concat_axis=0, tiled=True)  30.7 us
    all_to_all x1, waiting for transfers between devices, on_device(): lax.all_to_all(mixture, EP, split_axis=0, concat_axis=1, tiled=True)  28.5 us
    dot_general x4, matrix products, block_mix(): jnp.einsum('hts,she->the', mixing, value_heads, preferred_element_type=jn...  26.3 us
    all_to_all x1, waiting for transfers between devices, on_device(): lax.all_to_all(keys, EP, split_axis=1, concat_axis=0, tiled=True)  25.8 us
    all_to_all x1, waiting for transfers between devices, on_device(): lax.all_to_all(owned_sums.reshape(ep_count, capacity, model_width).astype...  18.8 us
  transfers between devices with their start and end apart: 11, of which 8 were waited for; matrix products, arithmetic and copies ran while one was open for 32% of the time, Pallas kernels for 0%

commit v1 on v0

--- a/solution.py
+++ b/solution.py
@@ -156,7 +156,10 @@
     arrived = lax.all_to_all(outgoing, EP, split_axis=0, concat_axis=0, tiled=True).reshape(
         ep_count * capacity, model_width
     )
-    gathered = lax.all_gather(arrived, "seg", axis=0, tiled=True)
+    b_next = lax.all_to_all(
+        jnp.stack([arrived] * lax.axis_size("seg")), axis_name="seg", split_axis=0, concat_axis=0
+    )
+    gathered = jnp.concatenate(b_next, 0)
     owned_sums = lax.psum_scatter(
         expert_output(gathered, up_piece, down_piece).astype(jnp.bfloat16),
         "seg",

time: 524 us -> 557 us (1.063)
  blocking collectives: 44.5 us -> 122 us
  waiting for transfers between devices: 196 us -> 155 us
    all_to_all x0 -> x1, blocking collectives: none -> 77.4 us  [on_device(): lax.all_to_all(jnp.stack([arrived] * lax.axis_size('seg')), axis_name='se...]
    all_gather x1 -> x0, waiting for transfers between devices: 40.3 us -> none  [on_device(): gathered = lax.all_gather(arrived, 'seg', axis=0, tiled=True)]
  transfers between devices with their start and end apart: 11 -> 10, of which waited for: 8 -> 7; matrix products, arithmetic and copies ran while one was open for 32% -> 30% of each run, Pallas kernels for 0% -> 0%
where the time goes in v1:
time: 557 us; the launch traced here: 554 us
  waiting for transfers between devices  155 us (28%)
  blocking collectives  122 us (22%)
  local copies, waits for them, and re-layouts  117 us (21%)
  matrix products  54.1 us (10%)
  starting transfers between devices  48.9 us (9%)
  other arithmetic  36.2 us (6%)
  between operations  14 us (3%)
  loops' own time  6.62 us (1%)
    all_to_all x1, blocking collectives, on_device(): lax.all_to_all(jnp.stack([arrived] * lax.axis_size('seg')), axis_name='se...  77.4 us
    reduce_scatter x2, waiting for transfers between devices, scatter_axes(): x = lax.psum_scatter(x, axis, scatter_dimension=dim, tiled=True)  61.8 us
    dynamic_update_slice x8, local copies, waits for them, and re-layouts, on_device(): lax.map(block_mix, starts).reshape(seg_length, heads_local, head_dim)  52.2 us
    all_to_all x1, blocking collectives, on_device(): lax.all_to_all(outgoing, EP, split_axis=0, concat_axis=0, tiled=True)  30.7 us
    all_to_all x1, waiting for transfers between devices, on_device(): lax.all_to_all(mixture, EP, split_axis=0, concat_axis=1, tiled=True)  27.7 us
    dot_general x4, matrix products, block_mix(): jnp.einsum('hts,she->the', mixing, value_heads, preferred_element_type=jn...  26.3 us
    all_to_all x1, waiting for transfers between devices, on_device(): lax.all_to_all(keys, EP, split_axis=1, concat_axis=0, tiled=True)  25.8 us
    all_to_all x1, waiting for transfers between devices, on_device(): lax.all_to_all(owned_sums.reshape(ep_count, capacity, model_width).astype...  18.8 us
  transfers between devices with their start and end apart: 10, of which 7 were waited for; matrix products, arithmetic and copies ran while one was open for 30% of the time, Pallas kernels for 0%

profile of v1, /device:TPU:2, one launch (start us, length us, event | category | flops | bytes accessed | tf_op | source)
XLA Modules:
  0.0 553.8 jit_solution(17855462094516664908)
XLA Ops:
  7.2 2.5 copy.199
  9.7 11.8 %all-to-all-start.1 = ((bf16[64,32,256]{2,0,1:T(8,128)(2,1)}), bf16[64,32,256]{2,0,1:T(8,128)(2,1)}, u32[]{:S(2)}, u32[]{:S(2)}) async-start(bf16[64,32,256]{2,0,1:T(8,128)(2,1)} %bitcast.114), calls=%async_computation.1 | async-start | bytes 2097152 | tf_op jit(solution)/shard_map/all_to_all | solution.py:70
  21.5 2.3 copy.198
  23.8 25.8 %all-to-all-done.1 = bf16[64,32,256]{2,0,1:T(8,128)(2,1)} async-done(((bf16[64,32,256]{2,0,1:T(8,128)(2,1)}), bf16[64,32,256]{2,0,1:T(8,128)(2,1)}, u32[]{:S(2)}, u32[]{:S(2)}) %all-to-all-start.1) | async-done | bytes 1048608 | tf_op jit(solution)/shard_map/all_to_all | solution.py:70
  49.6 5.6 %all-to-all-start.2 = ((bf16[64,32,256]{2,0,1:T(8,128)(2,1)}), bf16[64,32,256]{2,0,1:T(8,128)(2,1)}, u32[]{:S(2)}, u32[]{:S(2)}) async-start(bf16[64,32,256]{2,0,1:T(8,128)(2,1)} %bitcast.112), calls=%async_computation.2 | async-start | bytes 2097152 | tf_op jit(solution)/shard_map/all_to_all | solution.py:71
  64.1 2.3 copy.200
  67.8 2.2 reshape.158
  70.0 12.2 %all-to-all-done.2 = bf16[64,32,256]{2,0,1:T(8,128)(2,1)} async-done(((bf16[64,32,256]{2,0,1:T(8,128)(2,1)}), bf16[64,32,256]{2,0,1:T(8,128)(2,1)}, u32[]{:S(2)}, u32[]{:S(2)}) %all-to-all-start.2) | async-done | bytes 1048608 | tf_op jit(solution)/shard_map/all_to_all | solution.py:71
  82.3 5.6 %all-to-all-start = ((bf16[64,32,256]{2,0,1:T(8,128)(2,1)}), bf16[64,32,256]{2,0,1:T(8,128)(2,1)}, u32[]{:S(2)}, u32[]{:S(2)}) async-start(bf16[64,32,256]{2,0,1:T(8,128)(2,1)} %bitcast.113), calls=%async_computation | async-start | bytes 2097152 | tf_op jit(solution)/shard_map/all_to_all | solution.py:69
  87.9 2.2 reshape.161
  90.1 5.6 %convert_multiply_fusion.1 = bf16[2048,2,128]{2,1,0:T(2,128)(2,1)S(1)} fusion(bf16[2048,2,128]{2,1,0:T(2,128)(2,1)} %reshape.158, f32[2048,2]{1,0:T(8,128)} %copy.139), kind=kLoop, calls=%fused_computation.27 | loop fusion | flops 1572864 | bytes 2113536 | tf_op jit(solution)/shard_map/sh,shd,she->hde/dot_general | solution.py:101
  95.7 2.5 fusion.18
  100.7 13.8 %all_gather.6 = bf16[8,2,16385]{2,1,0:T(2,128)(2,1)S(1)} all-gather(bf16[1,2,16385]{2,1,0:T(2,128)(2,1)S(1)} %pad_maximum_fusion), channel_id=1, replica_groups=mesh['seg'=8,'ep_0'=8,'ep_1'=4] {'seg'}, dimensions={0}, use_global_device_ids=true | all-gather | bytes 589860 | tf_op jit(solution)/shard_map/all_gather | solution.py:16
  116.0 2.4 copy.136
  120.3 2.2 reshape.165
  122.6 2.1 reshape.157
  124.7 2.3 copy.135
  127.0 99.5 %while.11 = (s32[]{:T(128)}, f32[4,512,2,128]{1,0,3,2:T(4,128)}, s32[4]{0:T(128)S(1)}, bf16[2048,2,128]{2,0,1:T(8,128)(2,1)}, bf16[2048,2,128]{2,0,1:T(8,128)(2,...) while((s32[]{:T(128)}, f32[4,512,2,128]{1,0,3,2:T(4,128)}, ...), condition=%wide.region_3.4_spmd.clone, body=%wide.region_2.3_spmd.clone.sunk | while | flops 1085276672 | bytes 7110819 | solution.py:96
  132.3 6.6 %fusion.58 = f32[1,512,2,128]{3,1,2,0:T(8,128)} fusion(bf16[2048,2,128]{2,0,1:T(8,128)(2,1)} %get-tuple-element.204, bf16[2048,2,128]{2,0,1:T(8,128)(2,1)} %get-tuple-element.202, f32[2,2048]{1,0:T(2,128)} %get-tuple-element.203, f32[2,512]{1,0:T(2,128)S(1)} %constant_dynamic-slice_fusion.2, pred[512,2048]{1,0:T(8,128)(4,1)} %iota_compare_fusion.5, ...), kind=kOutput, calls=%fused_computation.4.clone.1 | convolution fusion | flops 1084227584 | bytes 3952644 | tf_op jit(solution)/shard_map/while/body/eval_jaxpr/hts,she->the/dot_general | solution.py:94
  140.8 11.1 %dynamic_update_slice.6 = f32[4,512,2,128]{1,0,3,2:T(4,128)} dynamic-update-slice(f32[4,512,2,128]{1,0,3,2:T(4,128)} %get-tuple-element.189, f32[1,512,2,128]{1,0,3,2:T(1,128)} %copy.204, s32[]{:T(128)} %get-tuple-element.188, s32[]{:T(128)} %constant.22.clone.1..sunk, s32[]{:T(128)} %constant.22.clone.1..sunk, s32[]{:T(128)} %constant.22.clone.1..sunk) | dynamic-update-slice | bytes 1048580 | tf_op jit(solution)/shard_map/while/body/jit(dynamic_update_index_in_dim)/dynamic_update_slice | solution.py:96
  157.2 6.6 %fusion.58 = f32[1,512,2,128]{3,1,2,0:T(8,128)} fusion(bf16[2048,2,128]{2,0,1:T(8,128)(2,1)} %get-tuple-element.204, bf16[2048,2,128]{2,0,1:T(8,128)(2,1)} %get-tuple-element.202, f32[2,2048]{1,0:T(2,128)} %get-tuple-element.203, f32[2,512]{1,0:T(2,128)S(1)} %constant_dynamic-slice_fusion.2, pred[512,2048]{1,0:T(8,128)(4,1)} %iota_compare_fusion.5, ...), kind=kOutput, calls=%fused_computation.4.clone.1 | convolution fusion | flops 1084227584 | bytes 3952644 | tf_op jit(solution)/shard_map/while/body/eval_jaxpr/hts,she->the/dot_general | solution.py:94
  165.7 11.1 %dynamic_update_slice.6 = f32[4,512,2,128]{1,0,3,2:T(4,128)} dynamic-update-slice(f32[4,512,2,128]{1,0,3,2:T(4,128)} %get-tuple-element.189, f32[1,512,2,128]{1,0,3,2:T(1,128)} %copy.204, s32[]{:T(128)} %get-tuple-element.188, s32[]{:T(128)} %constant.22.clone.1..sunk, s32[]{:T(128)} %constant.22.clone.1..sunk, s32[]{:T(128)} %constant.22.clone.1..sunk) | dynamic-update-slice | bytes 1048580 | tf_op jit(solution)/shard_map/while/body/jit(dynamic_update_index_in_dim)/dynamic_update_slice | solution.py:96
  182.0 6.6 %fusion.58 = f32[1,512,2,128]{3,1,2,0:T(8,128)} fusion(bf16[2048,2,128]{2,0,1:T(8,128)(2,1)} %get-tuple-element.204, bf16[2048,2,128]{2,0,1:T(8,128)(2,1)} %get-tuple-element.202, f32[2,2048]{1,0:T(2,128)} %get-tuple-element.203, f32[2,512]{1,0:T(2,128)S(1)} %constant_dynamic-slice_fusion.2, pred[512,2048]{1,0:T(8,128)(4,1)} %iota_compare_fusion.5, ...), kind=kOutput, calls=%fused_computation.4.clone.1 | convolution fusion | flops 1084227584 | bytes 3952644 | tf_op jit(solution)/shard_map/while/body/eval_jaxpr/hts,she->the/dot_general | solution.py:94
  190.5 11.1 %dynamic_update_slice.6 = f32[4,512,2,128]{1,0,3,2:T(4,128)} dynamic-update-slice(f32[4,512,2,128]{1,0,3,2:T(4,128)} %get-tuple-element.189, f32[1,512,2,128]{1,0,3,2:T(1,128)} %copy.204, s32[]{:T(128)} %get-tuple-element.188, s32[]{:T(128)} %constant.22.clone.1..sunk, s32[]{:T(128)} %constant.22.clone.1..sunk, s32[]{:T(128)} %constant.22.clone.1..sunk) | dynamic-update-slice | bytes 1048580 | tf_op jit(solution)/shard_map/while/body/jit(dynamic_update_index_in_dim)/dynamic_update_slice | solution.py:96
  206.9 6.6 %fusion.58 = f32[1,512,2,128]{3,1,2,0:T(8,128)} fusion(bf16[2048,2,128]{2,0,1:T(8,128)(2,1)} %get-tuple-element.204, bf16[2048,2,128]{2,0,1:T(8,128)(2,1)} %get-tuple-element.202, f32[2,2048]{1,0:T(2,128)} %get-tuple-element.203, f32[2,512]{1,0:T(2,128)S(1)} %constant_dynamic-slice_fusion.2, pred[512,2048]{1,0:T(8,128)(4,1)} %iota_compare_fusion.5, ...), kind=kOutput, calls=%fused_computation.4.clone.1 | convolution fusion | flops 1084227584 | bytes 3952644 | tf_op jit(solution)/shard_map/while/body/eval_jaxpr/hts,she->the/dot_general | solution.py:94
  215.4 11.1 %dynamic_update_slice.6 = f32[4,512,2,128]{1,0,3,2:T(4,128)} dynamic-update-slice(f32[4,512,2,128]{1,0,3,2:T(4,128)} %get-tuple-element.189, f32[1,512,2,128]{1,0,3,2:T(1,128)} %copy.204, s32[]{:T(128)} %get-tuple-element.188, s32[]{:T(128)} %constant.22.clone.1..sunk, s32[]{:T(128)} %constant.22.clone.1..sunk, s32[]{:T(128)} %constant.22.clone.1..sunk) | dynamic-update-slice | bytes 1048580 | tf_op jit(solution)/shard_map/while/body/jit(dynamic_update_index_in_dim)/dynamic_update_slice | solution.py:96
  226.5 3.7 reshape.162
  233.2 3.4 fusion.14
  236.6 3.7 copy.145
  240.3 2.5 reshape_reshape.3
  245.6 9.8 %all-to-all-start.4 = ((f32[32,1,256]{2,1,0:T(1,128)}), f32[32,1,256]{2,1,0:T(1,128)}, u32[]{:S(2)}, u32[]{:S(2)}) async-start(f32[32,1,256]{2,1,0:T(1,128)} %broadcast_in_dim.85), calls=%async_computation.4 | async-start | bytes 65536 | tf_op jit(solution)/shard_map/all_to_all | solution.py:26
  256.3 7.8 %all-to-all-done.4 = f32[32,1,256]{2,1,0:T(1,128)} async-done(((f32[32,1,256]{2,1,0:T(1,128)}), f32[32,1,256]{2,1,0:T(1,128)}, u32[]{:S(2)}, u32[]{:S(2)}) %all-to-all-start.4) | async-done | bytes 32800 | tf_op jit(solution)/shard_map/all_to_all | solution.py:26
  265.0 4.7 convolution_convert_fusion.1
  269.8 41.9 %reduce-scatter.4.cloned.1.call-done = bf16[32,6144]{1,0:T(8,128)(2,1)} async-done(((bf16[256,6144]{1,0:T(8,128)(2,1)}), bf16[32,6144]{1,0:T(8,128)(2,1)}) %reduce-scatter.4.cloned.1.call-update) | async-done | bytes 393232 | tf_op jit(solution)/shard_map/reduce_scatter | solution.py:35
  315.2 19.9 %reduce-scatter.6.cloned.1.call-done = bf16[8,6144]{1,0:T(8,128)(2,1)} async-done(((bf16[32,6144]{1,0:T(8,128)(2,1)}), bf16[8,6144]{1,0:T(8,128)(2,1)}) %reduce-scatter.6.cloned.1.call-update) | async-done | bytes 98320 | tf_op jit(solution)/shard_map/reduce_scatter | solution.py:35
  337.0 2.0 reshape.166
  340.4 30.7 %all_to_all.82 = bf16[32,2,6144]{2,1,0:T(2,128)(2,1)} all-to-all(bf16[32,2,6144]{2,1,0:T(2,128)(2,1)S(1)} %bitcast.115), channel_id=1, replica_groups=mesh['seg'=8,'ep_0'=8,'ep_1'=4] {'ep_0','ep_1'}, dimensions={0} | all-to-all | bytes 1572864 | tf_op jit(solution)/shard_map/all_to_all | solution.py:156
  371.2 3.0 stack_reshape.2
  376.0 77.4 %all_to_all.83 = bf16[8,64,6144]{2,1,0:T(8,128)(2,1)} all-to-all(bf16[8,64,6144]{2,1,0:T(8,128)(2,1)S(1)} %stack.3), channel_id=1, replica_groups=mesh['seg'=8,'ep_0'=8,'ep_1'=4] {'seg'}, dimensions={0} | all-to-all | bytes 12582912 | tf_op jit(solution)/shard_map/all_to_all | solution.py:159
  453.4 12.0 %convolution_convert_fusion = bf16[512,6144]{1,0:T(8,128)(2,1)} fusion(bf16[1,288,6144]{2,1,0:T(8,128)(2,1)S(1)} %copy-done, bf16[512,6144]{1,0:T(8,128)(2,1)} %bitcast.110, bf16[1,6144,288]{1,2,0:T(8,128)(2,1)} %param.20), kind=kOutput, calls=%fused_computation.10 | convolution fusion | flops 3627761664 | bytes 19660800 | tf_op jit(solution)/shard_map/dot_general | solution.py:59
  465.4 2.5 all_to_all.68
  468.0 5.6 %all-to-all-start.3 = ((bf16[32,64,256]{2,1,0:T(8,128)(2,1)}), bf16[32,64,256]{2,1,0:T(8,128)(2,1)}, u32[]{:S(2)}, u32[]{:S(2)}) async-start(bf16[32,64,256]{2,1,0:T(8,128)(2,1)} %all_to_all.68), calls=%async_computation.3 | async-start | bytes 2097152 | tf_op jit(solution)/shard_map/all_to_all | solution.py:124
  473.7 27.7 %all-to-all-done.3 = bf16[32,64,256]{2,1,0:T(8,128)(2,1)} async-done(((bf16[32,64,256]{2,1,0:T(8,128)(2,1)}), bf16[32,64,256]{2,1,0:T(8,128)(2,1)}, u32[]{:S(2)}, u32[]{:S(2)}) %all-to-all-start.3) | async-done | bytes 1048608 | tf_op jit(solution)/shard_map/all_to_all | solution.py:124
  506.0 2.9 convert_element_type.93
  508.8 10.0 %all-to-all-start.7 = ((bf16[32,2,6144]{2,1,0:T(2,128)(2,1)}), bf16[32,2,6144]{2,1,0:T(2,128)(2,1)}, u32[]{:S(2)}, u32[]{:S(2)}) async-start(bf16[32,2,6144]{2,1,0:T(2,128)(2,1)} %convert_element_type.93), calls=%async_computation.10 | async-start | bytes 1572864 | tf_op jit(solution)/shard_map/all_to_all | solution.py:169
  518.8 2.8 multiply_convert_fusion.1
  521.7 18.8 %all-to-all-done.7 = bf16[32,2,6144]{2,1,0:T(2,128)(2,1)} async-done(((bf16[32,2,6144]{2,1,0:T(2,128)(2,1)}), bf16[32,2,6144]{2,1,0:T(2,128)(2,1)}, u32[]{:S(2)}, u32[]{:S(2)}) %all-to-all-start.7) | async-done | bytes 786464 | tf_op jit(solution)/shard_map/all_to_all | solution.py:169
  540.4 2.0 convert.7
  (97 shorter events, 64.0 us)
Async XLA Ops:
  7.2 446.2 %copy-start = (bf16[1,288,6144]{2,1,0:T(8,128)(2,1)S(1)}, bf16[1,288,6144]{2,1,0:T(8,128)(2,1)}, u32[]{:S(2)}) copy-start(bf16[1,288,6144]{2,1,0:T(8,128)(2,1)} %param.21) | copy-start | bytes 10616836
  9.7 46.3 %copy-start.4 = (f32[2048,2]{0,1:T(2,128)S(1)}, f32[2048,2]{0,1:T(2,128)}, u32[]{:S(2)}) copy-start(f32[2048,2]{0,1:T(2,128)} %param.15) | copy-start | bytes 49156
  9.7 39.9 %all-to-all-start.1 = ((bf16[64,32,256]{2,0,1:T(8,128)(2,1)}), bf16[64,32,256]{2,0,1:T(8,128)(2,1)}, u32[]{:S(2)}, u32[]{:S(2)}) async-start(bf16[64,32,256]{2,0,1:T(8,128)(2,1)} %bitcast.114), calls=%async_computation.1 | async-start | bytes 2097152 | tf_op jit(solution)/shard_map/all_to_all | solution.py:70
  49.6 32.7 %all-to-all-start.2 = ((bf16[64,32,256]{2,0,1:T(8,128)(2,1)}), bf16[64,32,256]{2,0,1:T(8,128)(2,1)}, u32[]{:S(2)}, u32[]{:S(2)}) async-start(bf16[64,32,256]{2,0,1:T(8,128)(2,1)} %bitcast.112), calls=%async_computation.2 | async-start | bytes 2097152 | tf_op jit(solution)/shard_map/all_to_all | solution.py:71
  55.2 209.8 %all-gather.2.cloned.1.call-start = ((), (), s32[]{:S(2)}) async-start(), calls=%async_computation.11 | async-start | bytes 3538944 | tf_op jit(solution)/shard_map/all_gather | solution.py:140
  82.3 40.3 %all-to-all-start = ((bf16[64,32,256]{2,0,1:T(8,128)(2,1)}), bf16[64,32,256]{2,0,1:T(8,128)(2,1)}, u32[]{:S(2)}, u32[]{:S(2)}) async-start(bf16[64,32,256]{2,0,1:T(8,128)(2,1)} %bitcast.113), calls=%async_computation | async-start | bytes 2097152 | tf_op jit(solution)/shard_map/all_to_all | solution.py:69
  99.6 18.7 %copy-start.1 = (bf16[2048,2,128]{2,1,0:T(2,128)(2,1)S(1)}, bf16[2048,2,128]{2,1,0:T(2,128)(2,1)}, u32[]{:S(2)}) copy-start(bf16[2048,2,128]{2,1,0:T(2,128)(2,1)} %reshape.161) | copy-start | bytes 3145732
  119.6 7.4 %copy-start.7 = (bf16[8,2,1]{0,1,2:T(2,128)(2,1)}, bf16[8,2,1]{0,1,2:T(2,128)(2,1)S(1)}, u32[]{:S(2)}) copy-start(bf16[8,2,1]{0,1,2:T(2,128)(2,1)S(1)} %copy.159) | copy-start | bytes 100
  226.5 6.7 %copy-start.3 = (f32[2048,2]{0,1:T(2,128)S(1)}, f32[2048,2]{0,1:T(2,128)}, u32[]{:S(2)}) copy-start(f32[2048,2]{0,1:T(2,128)} %get-tuple-element.131) | copy-start | bytes 49156
  244.2 0.7 copy-start.2
  245.6 18.5 %all-to-all-start.4 = ((f32[32,1,256]{2,1,0:T(1,128)}), f32[32,1,256]{2,1,0:T(1,128)}, u32[]{:S(2)}, u32[]{:S(2)}) async-start(f32[32,1,256]{2,1,0:T(1,128)} %broadcast_in_dim.85), calls=%async_computation.4 | async-start | bytes 65536 | tf_op jit(solution)/shard_map/all_to_all | solution.py:26
  255.5 56.2 %reduce-scatter.4.cloned.1.call-start = ((), (), s32[]{:S(2)}) async-start(), calls=%async_computation.12 | async-start | bytes 3538944 | tf_op jit(solution)/shard_map/reduce_scatter | solution.py:35
  269.7 42.3 %copy-start.5 = (s32[8,2]{0,1:T(2,128)S(1)}, s32[8,2]{0,1:T(2,128)}, u32[]{:S(2)}) copy-start(s32[8,2]{0,1:T(2,128)} %param.18) | copy-start | bytes 196
  269.7 65.3 %reduce-scatter.6.cloned.1.call-start = ((), (), s32[]{:S(2)}) async-start(), calls=%async_computation.13 | async-start | bytes 491520 | tf_op jit(solution)/shard_map/reduce_scatter | solution.py:35
  311.7 194.3 %reduce-scatter.8.cloned.1.call-start = ((), (), s32[]{:S(2)}) async-start(), calls=%async_computation.14 | async-start | bytes 7077888 | tf_op jit(solution)/shard_map/reduce_scatter | solution.py:163
  465.4 8.2 %copy-start.6 = (f32[8,2]{0,1:T(2,128)S(1)}, f32[8,2]{0,1:T(2,128)}, u32[]{:S(2)}) copy-start(f32[8,2]{0,1:T(2,128)} %param.19) | copy-start | bytes 196
  468.0 33.4 %all-to-all-start.3 = ((bf16[32,64,256]{2,1,0:T(8,128)(2,1)}), bf16[32,64,256]{2,1,0:T(8,128)(2,1)}, u32[]{:S(2)}, u32[]{:S(2)}) async-start(bf16[32,64,256]{2,1,0:T(8,128)(2,1)} %all_to_all.68), calls=%async_computation.3 | async-start | bytes 2097152 | tf_op jit(solution)/shard_map/all_to_all | solution.py:124
  508.8 31.6 %all-to-all-start.7 = ((bf16[32,2,6144]{2,1,0:T(2,128)(2,1)}), bf16[32,2,6144]{2,1,0:T(2,128)(2,1)}, u32[]{:S(2)}, u32[]{:S(2)}) async-start(bf16[32,2,6144]{2,1,0:T(2,128)(2,1)} %convert_element_type.93), calls=%async_computation.10 | async-start | bytes 1572864 | tf_op jit(solution)/shard_map/all_to_all | solution.py:169
Sparse Core Ops, SparseCore 0:
  57.9 31.4 all-gather.1
  269.8 41.8 reduce-scatter.3
  314.2 20.7 reduce-scatter.5
  465.6 40.2 reduce-scatter.7
